TPU v7x, 32 devices: a whole 2x2x4 slice. The times are simulated.
32 devices in a mesh: phonon: 2 (over y), row: 4 (over x, core), beam: 4 (over z).
Axes of the slice: x: 2, y: 2, z: 4, core: 2. Of those that a mesh axis runs over, the one named last changes fastest.
Arguments:
- spectra: float32 [2, 8, 512, 512], P(None, ('phonon', 'beam'), 'row'), parts along dimension 1, may hold values from -6 to 6
- potential: float32 [1024, 512], P(('phonon', 'beam'), 'row'), parts along dimension 0, may hold values from -3.140625 to 3.140625
- amp_re: float32 [4], replicated, may hold values from -0.75 to 0.75
- amp_im: float32 [4], replicated, may hold values from -0.75 to 0.75
- beam_freq: int32 [4, 2], replicated, may hold values from -32 to 31
- probe_corners: int32 [16, 2], replicated, may hold values from 0 to 511, as said below
- slot_table: int32 [4, 4, 2], replicated, may hold values from 0 to 16, as said below
Outputs:
- patterns: float32 [8, 4, 2, 128, 128], P(('phonon', 'beam'), 'row'), parts along dimension 0
There are 2 independent parts, one for each index of `phonon`. A program takes and returns all parts, laid end to end along the dimension named above; an argument that names none is the same for every part. Nothing has to cross between parts.
Inputs may be any that keep to these rules, and one draw needn't show every extreme that they name: `probe_corners`: the corner of each probe lies in the tile (corner row // 128, corner column // 128) whose list in slot_table names that probe. slot_table[i, j] lists in rising order the probes whose window corner lies in tile rows i * 128 to (i + 1) * 128 - 1 and columns j * 128 to (j + 1) * 128 - 1, then the value 16 in every unused slot; each probe is listed exactly once; in every draw some tile lists 2 probes.
All inputs are finite; a program needn't handle non-finite values.
Results may differ from a plain program's by a relative error of at most 0.0003.
Values sent between devices are 32-bit elements; how exact they have to be, the bound alone decides.
No kernel may reach another device: no remote copies, remote signals or barrier semaphores. Data moves between devices by JAX's collectives and lax.ppermute only.
A program may use at most 64 MiB of HBM per device.

v0:
```python
import functools
import math

import jax
import jax.numpy as jnp
import numpy as np
from jax import lax
from jax.experimental import pallas as pl
from jax.experimental.pallas import tpu as pltpu
from jax.sharding import PartitionSpec as P

WIN = 128

prop_coef = 3e-05
f32, bf16 = jnp.float32, jnp.bfloat16


def shift(shard, axis, by):
    devices = lax.axis_size(axis)
    return lax.ppermute(shard, axis, [(i, (i + by) % devices) for i in range(devices)])


def split_table(table):
    high = np.asarray(table, np.float32).astype(bf16)
    low = (np.asarray(table, np.float64) - high.astype(np.float64)).astype(np.float32).astype(bf16)
    return high, low


def wave_table(length):
    index = np.arange(length)
    freq = np.where(index < length // 2, index, index - length).astype(np.float64)
    turns = (index[:, None] * index[None, :]) % length
    angle = 2.0 * math.pi / length * turns - prop_coef * (freq * freq)[:, None]
    return np.cos(angle) / math.sqrt(length), np.sin(angle) / math.sqrt(length)


def row_tables(length, tile_cols, tiles):
    real, imag = wave_table(length)
    cols = (np.arange(tiles)[:, None] * tile_cols + np.arange(WIN)[None, :]) % length
    both = np.concatenate([real[:, cols], imag[:, cols]], axis=2)
    return split_table(np.moveaxis(both, 1, 0))


def column_tables(length):
    radix = length // WIN
    real, imag = wave_table(length)
    parts = []
    for k0 in range(radix):
        both = np.concatenate([real[k0::radix, :WIN].T, imag[k0::radix, :WIN].T], axis=0)
        high, low = split_table(both)
        parts.append(np.concatenate([high, low, high], axis=1))
    return np.stack(parts)


def window_tables():
    index = np.arange(WIN)
    angle = -2.0 * math.pi / WIN * ((index[:, None] * index[None, :]) % WIN)
    real, imag = np.cos(angle) / math.sqrt(WIN), np.sin(angle) / math.sqrt(WIN)
    left = np.concatenate([np.concatenate([real, -imag], 1), np.concatenate([imag, real], 1)], 0)
    right = np.concatenate([np.concatenate([real, imag], 1), np.concatenate([-imag, real], 1)], 0)
    return split_table(left) + split_table(right)


def split(value):
    high = value.astype(bf16)
    return high, (value - high.astype(f32)).astype(bf16)


def mul(left, right):
    return jnp.dot(left, right, preferred_element_type=f32)


def row_kernel(tiles, step, spectra, high, low, *messages):
    me = lax.axis_index("row")
    rows = spectra.shape[2]
    lhs = jnp.concatenate([spectra[0, 0], spectra[1, 0]], axis=0)
    lhs_high, lhs_low = split(lhs)
    for k in range(tiles):
        tile = lax.rem(me + k, tiles)
        table = high[tile]
        both = mul(lhs_high, table) + mul(lhs_low, table) + mul(lhs_high, low[tile])
        real = both[:rows, :WIN] - both[rows:, WIN:]
        imag = both[:rows, WIN:] + both[rows:, :WIN]
        for block, to in enumerate((k, (k - step) % tiles)):
            messages[to][block, 0] = real
            messages[to][block, 1] = imag


def prep_kernel(sizes, slots_ref, corners, freq, amp_re, amp_im, cosine, sine, params):
    row_tiles, col_tiles, slots, probes, tile_rows, tile_cols, grid_len = sizes
    beam_pos, row_pos = lax.axis_index("beam"), lax.axis_index("row")
    for k in range(row_tiles):
        tile = lax.rem(beam_pos + k, row_tiles)
        for s in range(slots):
            probe = slots_ref[(tile * col_tiles + row_pos) * slots + s]
            live = (probe < probes).astype(f32)
            safe = jnp.minimum(probe, probes - 1)
            top, left = corners[2 * safe], corners[2 * safe + 1]
            turns = lax.rem(top * freq[2 * beam_pos] + left * freq[2 * beam_pos + 1], grid_len)
            turns = lax.rem(turns + grid_len, grid_len)
            re, im = amp_re[beam_pos] * live, amp_im[beam_pos] * live
            c, n = cosine[turns], sine[turns]
            values = [
                re * c - im * n,
                re * n + im * c,
                jnp.clip(top - tile * tile_rows, 0, tile_rows - 1).astype(f32),
                jnp.clip(left - row_pos * tile_cols, 0, tile_cols - 1).astype(f32),
            ]
            for at, value in enumerate(values):
                params[k * slots + s, at] = jnp.full((WIN,), value, f32)


def masks_of(params, at):
    row = lax.broadcasted_iota(jnp.int32, (WIN, WIN), 0).astype(f32)
    col = lax.broadcasted_iota(jnp.int32, (WIN, WIN), 1).astype(f32)
    return row >= params[at, 2:3, :], col >= params[at, 3:4, :]


def pick(rows_here, cols_here, near_near, near_far, far_near, far_far):
    return jnp.where(
        rows_here,
        jnp.where(cols_here, near_near, near_far),
        jnp.where(cols_here, far_near, far_far),
    )


def transmit_kernel(slots, phase, params, out):
    for s in range(slots):
        rows_here, cols_here = masks_of(params, s)
        value = pick(
            rows_here,
            cols_here,
            phase[:WIN, :WIN],
            phase[:WIN, WIN:],
            phase[WIN:, :WIN],
            phase[WIN:, WIN:],
        )
        out[s, :, :WIN] = jnp.cos(value)
        out[s, :, WIN:] = jnp.sin(value)


def column_kernel(sizes, *refs):
    sources, radix, row_tiles, slots, tile_rows = sizes
    arrived, (table, params) = refs[:sources], refs[sources : sources + 2]
    sends = refs[sources + 2 : sources + 2 + row_tiles]
    gathered, waves = refs[sources + 2 + row_tiles :]
    row_pos, beam_pos = lax.axis_index("row"), lax.axis_index("beam")
    part = arrived[0].shape[2] // radix
    for k in range(sources):
        source = lax.rem(row_pos + sources - k, sources)
        at = pl.ds(pl.multiple_of(source * part, part), part)
        for k0 in range(radix):
            for block in range(2):
                for c in range(2):
                    cols = slice((2 * block + c) * WIN, (2 * block + c + 1) * WIN)
                    gathered[k0, at, cols] = arrived[k][
                        block, c, pl.ds(k0, part, stride=radix), :
                    ]
    pieces = []
    for k0 in range(radix):
        high, low = split(gathered[k0])
        both = mul(table[k0], jnp.concatenate([high, high, low], axis=0))
        halves = []
        for block in range(2):
            at = block * 2 * WIN
            real = both[:WIN, at : at + WIN] - both[WIN:, at + WIN : at + 2 * WIN]
            imag = both[:WIN, at + WIN : at + 2 * WIN] + both[WIN:, at : at + WIN]
            halves.append((real, imag))
        pieces.append(halves)
    grid_len = radix * WIN
    for block in range(2):
        at = block * 2 * WIN
        for a in range(radix):
            real = imag = None
            for k0 in range(radix):
                re, im = pieces[k0][block]
                quarter = (4 * k0 * a // radix) % 4
                re, im = [(re, im), (-im, re), (-re, -im), (im, -re)][quarter]
                real = re if real is None else real + re
                imag = im if imag is None else imag + im
            waves[a * WIN : (a + 1) * WIN, at : at + WIN] = real
            waves[a * WIN : (a + 1) * WIN, at + WIN : at + 2 * WIN] = imag
            if a == 0:
                waves[grid_len : grid_len + WIN, at : at + WIN] = real
                waves[grid_len : grid_len + WIN, at + WIN : at + 2 * WIN] = imag
    for k in range(row_tiles):
        start = lax.rem(beam_pos + k, row_tiles) * tile_rows
        near = pl.ds(pl.multiple_of(start, 8), WIN)
        far = pl.ds(pl.multiple_of(lax.rem(start + WIN, grid_len), 8), WIN)
        for s in range(slots):
            which = k * slots + s
            rows_here, cols_here = masks_of(params, which)
            picked = []
            for c in range(2):
                first = slice(c * WIN, (c + 1) * WIN)
                second = slice((c + 2) * WIN, (c + 3) * WIN)
                picked.append(
                    pick(
                        rows_here,
                        cols_here,
                        waves[near, first],
                        waves[near, second],
                        waves[far, first],
                        waves[far, second],
                    )
                )
            re, im = picked
            coef_re, coef_im = params[which, 0:1, :], params[which, 1:2, :]
            sends[k][s, :, :WIN] = re * coef_re - im * coef_im
            sends[k][s, :, WIN:] = re * coef_im + im * coef_re


def pattern_kernel(sources, slots, *refs):
    arrived = refs[:sources]
    transmit, left_high, left_low, right_high, right_low, out = refs[sources:]
    tops, bottoms = [], []
    for s in range(slots):
        total = arrived[0][s]
        for k in range(1, sources):
            total = total + arrived[k][s]
        re, im = total[:, :WIN], total[:, WIN:]
        t_re, t_im = transmit[s, :, :WIN], transmit[s, :, WIN:]
        tops.append(re * t_re - im * t_im)
        bottoms.append(re * t_im + im * t_re)
    window = jnp.concatenate(
        [jnp.concatenate(tops, axis=1), jnp.concatenate(bottoms, axis=1)], axis=0
    )
    high, low = split(window)
    inner = mul(left_high[...], high) + mul(left_high[...], low) + mul(left_low[...], high)
    inner = jnp.concatenate(
        [
            jnp.concatenate(
                [inner[:WIN, s * WIN : (s + 1) * WIN], inner[WIN:, s * WIN : (s + 1) * WIN]], axis=1
            )
            for s in range(slots)
        ],
        axis=0,
    )
    high, low = split(inner)
    outer = mul(high, right_high[...]) + mul(low, right_high[...]) + mul(high, right_low[...])
    power = outer[:, :WIN] * outer[:, :WIN] + outer[:, WIN:] * outer[:, WIN:]
    for s in range(slots):
        out[0, 0, s] = power[s * WIN : (s + 1) * WIN]


def call(kernel, name, ins, outs, smem=(), scratch=(), flops=0, moved=0):
    vmem, scalar = pl.BlockSpec(memory_space=pltpu.VMEM), pl.BlockSpec(memory_space=pltpu.SMEM)
    return pl.pallas_call(
        kernel,
        name=name,
        out_shape=outs,
        in_specs=[scalar if at in smem else vmem for at in range(len(ins))],
        out_specs=jax.tree.map(lambda _: vmem, outs),
        scratch_shapes=list(scratch),
        cost_estimate=pl.CostEstimate(flops=flops, bytes_accessed=moved, transcendentals=0),
    )(*ins)


def local(spectra, potential, amp_re, amp_im, beam_freq, probe_corners, slot_table):
    ky_rows, grid_len = spectra.shape[2], spectra.shape[3]
    tile_rows, tile_cols = potential.shape
    row_tiles, col_tiles, slots = slot_table.shape
    probes = probe_corners.shape[0]
    radix = grid_len // WIN

    def floats(*shape):
        return jax.ShapeDtypeStruct(shape, f32)

    row_high, row_low = row_tables(grid_len, tile_cols, col_tiles)
    messages = call(
        functools.partial(row_kernel, col_tiles, WIN // tile_cols),
        "row_transform",
        (spectra, jnp.asarray(row_high), jnp.asarray(row_low)),
        [floats(2, 2, ky_rows, WIN)] * col_tiles,
        flops=24 * ky_rows * grid_len * WIN * col_tiles,
        moved=8 << 20,
    )
    arrived = [messages[0]] + [shift(messages[k], "row", k) for k in range(1, col_tiles)]

    index = np.arange(grid_len)
    angle = -2.0 * math.pi / grid_len * index
    params = call(
        functools.partial(
            prep_kernel,
            (row_tiles, col_tiles, slots, probes, tile_rows, tile_cols, grid_len),
        ),
        "slot_parameters",
        (
            slot_table.reshape(-1),
            probe_corners.reshape(-1),
            beam_freq.reshape(-1),
            amp_re,
            amp_im,
            jnp.asarray(np.cos(angle), f32),
            jnp.asarray(np.sin(angle), f32),
        ),
        floats(row_tiles * slots, 8, WIN),
        smem=range(7),
    )

    below = [potential] + [shift(potential, "beam", -k) for k in range(1, WIN // tile_rows + 1)]
    tall = jnp.concatenate(below, axis=0)
    beside = [tall] + [shift(tall, "row", -k) for k in range(1, WIN // tile_cols + 1)]
    phase = jnp.concatenate(beside, axis=1)
    phase = jnp.pad(phase, [(0, 2 * WIN - length) for length in phase.shape])
    transmit = call(
        functools.partial(transmit_kernel, slots),
        "transmission",
        (phase, params),
        floats(slots, WIN, 2 * WIN),
    )

    sends = call(
        functools.partial(column_kernel, (col_tiles, radix, row_tiles, slots, tile_rows)),
        "column_transform",
        (*arrived, jnp.asarray(column_tables(grid_len)), params),
        [floats(slots, WIN, 2 * WIN)] * row_tiles,
        scratch=(
            pltpu.VMEM((radix, WIN, 4 * WIN), f32),
            pltpu.VMEM((grid_len + WIN, 4 * WIN), f32),
        ),
        flops=24 * grid_len * WIN * 2 * WIN,
        moved=4 << 20,
    )
    parts = [sends[0]] + [shift(sends[k], "beam", k) for k in range(1, row_tiles)]

    return call(
        functools.partial(pattern_kernel, row_tiles, slots),
        "patterns",
        (*parts, transmit, *(jnp.asarray(table) for table in window_tables())),
        floats(1, 1, slots, WIN, WIN),
        flops=48 * slots * WIN * WIN * WIN,
        moved=2 << 20,
    )


def solution(mesh):
    return jax.shard_map(
        local,
        mesh=mesh,
        in_specs=(
            P(None, ("phonon", "beam"), "row", None),
            P(("phonon", "beam"), "row"),
            P(),
            P(),
            P(),
            P(),
            P(),
        ),
        out_specs=P(("phonon", "beam"), "row", None, None, None),
        check_vma=False,
    )
```

profile of v0, /device:TPU:9, one launch (start us, length us, event | category | flops | bytes accessed | tf_op | source)
XLA Modules:
  0.0 52.0 jit_solution(6338793787318018319)
XLA Ops:
  0.0 3.6 %row_transform.1 = (f32[2,2,128,128]{3,2,1,0:T(8,128)}, f32[2,2,128,128]{3,2,1,0:T(8,128)}, f32[2,2,128,128]{3,2,1,0:T(8,128)}, f32[2,2,128,128]{3,2,1,0:T(8,128)}) custom-call(f32[2,1,128,512]{3,2,1,0:T(8,128)} %spectra.1, bf16[4,512,256]{2,1,0:T(8,128)(2,1)} %constant.9.clone.high, bf16[4,512,256]{2,1,0:T(8,128)(2,1)} %constant.20.clone.low), custom_call_target="tpu_custom_call" | custom-call | flops 805306368 | bytes 8388608 | tf_op jit(solution)/shard_map/row_transform/pallas_call | solution.py:248
  3.6 1.8 %collective-permute-start = (f32[2,2,128,128]{3,2,1,0:T(8,128)}, f32[2,2,128,128]{3,2,1,0:T(8,128)S(1)}, u32[]{:S(2)}, u32[]{:S(2)}) collective-permute-start(f32[2,2,128,128]{3,2,1,0:T(8,128)} %get-tuple-element.14), channel_id=1, source_target_pairs={{0,4},{4,8},{8,12},{12,0},{1,5},{5,9},{9,13},{13,1},{2,6},{6,10},{... | collective-permute-start | bytes 786440 | tf_op jit(solution)/shard_map/ppermute | solution.py:20
  5.4 0.3 collective-permute-start.1
  6.0 0.4 copy-done.8
  6.4 0.7 %reshape.10.corners = s32[32]{0:T(128)} reshape(s32[16,2]{1,0:T(8,128)S(1)} %copy.21) | data formatting | bytes 256 | tf_op jit(solution)/shard_map/reshape | solution.py:290
  7.2 0.6 %reshape.9.slots_ref = s32[32]{0:T(128)} reshape(s32[4,4,2]{2,1,0:T(4,128)S(1)} %copy.20) | data formatting | bytes 256 | tf_op jit(solution)/shard_map/reshape | solution.py:289
  8.0 0.6 %reshape.11.freq = s32[8]{0:T(128)} reshape(s32[4,2]{1,0:T(4,128)S(1)} %copy.22) | data formatting | bytes 64 | tf_op jit(solution)/shard_map/reshape | solution.py:291
  8.5 1.5 %slot_parameters.1.refs_5_.params = f32[8,8,128]{2,1,0:T(8,128)} custom-call(s32[32]{0:T(128)} %reshape.9.slots_ref, s32[32]{0:T(128)} %reshape.10.corners, s32[8]{0:T(128)} %reshape.11.freq, f32[4]{0:T(128)} %amp_re.1, f32[4]{0:T(128)} %amp_im.1, f32[512]{0:T(512)} %constant.21.clone.cosine, f32[512]{0:T(512)} %constant.22.clone.sine), custom_call_target="tpu_custom_call" | custom-call | tf_op jit(solution)/shard_map/slot_parameters/pallas_call | solution.py:248
  10.1 1.2 %collective-permute-done.refs_1_ = f32[2,2,128,128]{3,2,1,0:T(8,128)S(1)} collective-permute-done((f32[2,2,128,128]{3,2,1,0:T(8,128)}, f32[2,2,128,128]{3,2,1,0:T(8,128)S(1)}, u32[]{:S(2)}, u32[]{:S(2)}) %collective-permute-start) | collective-permute-done | bytes 262176 | tf_op jit(solution)/shard_map/ppermute | solution.py:20
  11.2 6.2 %collective-permute-done.1.refs_2_ = f32[2,2,128,128]{3,2,1,0:T(8,128)S(1)} collective-permute-done((f32[2,2,128,128]{3,2,1,0:T(8,128)}, f32[2,2,128,128]{3,2,1,0:T(8,128)S(1)}, u32[]{:S(2)}, u32[]{:S(2)}) %collective-permute-start.1) | collective-permute-done | bytes 262176 | tf_op jit(solution)/shard_map/ppermute | solution.py:20
  17.4 0.6 %collective-permute-done.2.refs_3_ = f32[2,2,128,128]{3,2,1,0:T(8,128)S(1)} collective-permute-done((f32[2,2,128,128]{3,2,1,0:T(8,128)}, f32[2,2,128,128]{3,2,1,0:T(8,128)S(1)}, u32[]{:S(2)}, u32[]{:S(2)}) %collective-permute-start.2) | collective-permute-done | bytes 262176 | tf_op jit(solution)/shard_map/ppermute | solution.py:20
  18.2 0.6 %copy-done.4 = f32[2,2,128,128]{3,2,1,0:T(8,128)} copy-done((f32[2,2,128,128]{3,2,1,0:T(8,128)}, f32[2,2,128,128]{3,2,1,0:T(8,128)S(1)}, u32[]{:S(2)}) %copy-start.4) | copy-done | bytes 262168
  18.7 3.5 %column_transform.1 = (f32[2,128,256]{2,1,0:T(8,128)}, f32[2,128,256]{2,1,0:T(8,128)}, f32[2,128,256]{2,1,0:T(8,128)}, f32[2,128,256]{2,1,0:T(8,128)}) custom-call(f32[2,2,128,128]{3,2,1,0:T(8,128)} %get-tuple-element.13.refs_0_, f32[2,2,128,128]{3,2,1,0:T(8,128)} %copy-done, f32[2,2,128,128]{3,2,1,0:T(8,128)} %copy-done.2, f32[2,2,128,128]{3,2,1,0:T(8,128)} %copy-done.4, ...), custom_call_target="tpu_custom_call" | custom-call | flops 402653184 | bytes 4194304 | tf_op jit(solution)/shard_map/column_transform/pallas_call | solution.py:248
  22.3 1.3 %collective-permute-start.3 = (f32[2,128,256]{2,1,0:T(8,128)}, f32[2,128,256]{2,1,0:T(8,128)S(1)}, u32[]{:S(2)}, u32[]{:S(2)}) collective-permute-start(f32[2,128,256]{2,1,0:T(8,128)} %get-tuple-element.18), channel_id=1, source_target_pairs={{0,1},{1,2},{2,3},{3,0},{4,5},{5,6},{6,7},{7,4},{8,9},{9,10},{10,1... | collective-permute-start | bytes 786440 | tf_op jit(solution)/shard_map/ppermute | solution.py:20
  23.5 1.0 %collective-permute-start.4 = (f32[2,128,256]{2,1,0:T(8,128)}, f32[2,128,256]{2,1,0:T(8,128)S(1)}, u32[]{:S(2)}, u32[]{:S(2)}) collective-permute-start(f32[2,128,256]{2,1,0:T(8,128)} %get-tuple-element.19), channel_id=1, source_target_pairs={{0,2},{1,3},{2,0},{3,1},{4,6},{5,7},{6,4},{7,5},{8,10},{9,11},{10,... | collective-permute-start | bytes 786440 | tf_op jit(solution)/shard_map/ppermute | solution.py:20
  24.6 1.5 %collective-permute-start.5 = (f32[2,128,256]{2,1,0:T(8,128)}, f32[2,128,256]{2,1,0:T(8,128)S(1)}, u32[]{:S(2)}, u32[]{:S(2)}) collective-permute-start(f32[2,128,256]{2,1,0:T(8,128)} %get-tuple-element.20), channel_id=1, source_target_pairs={{0,3},{1,0},{2,1},{3,2},{4,7},{5,4},{6,5},{7,6},{8,11},{9,8},{10,9... | collective-permute-start | bytes 786440 | tf_op jit(solution)/shard_map/ppermute | solution.py:20
  26.1 0.7 %collective-permute-start.7 = (f32[256,128]{1,0:T(8,128)S(1)}, f32[256,128]{1,0:T(8,128)S(1)}, u32[]{:S(2)}, u32[]{:S(2)}) collective-permute-start(f32[256,128]{1,0:T(8,128)S(1)} %constant_dynamic-update-slice_fusion), channel_id=1, source_target_pairs={{0,12},{4,0},{8,4},{12,8},{1,13},{5,1},{9,5},{13,9},{2,14},{6,2},{... | collective-permute-start | bytes 393224 | tf_op jit(solution)/shard_map/ppermute | solution.py:20
  26.7 4.1 %collective-permute-done.7 = f32[256,128]{1,0:T(8,128)S(1)} collective-permute-done((f32[256,128]{1,0:T(8,128)S(1)}, f32[256,128]{1,0:T(8,128)S(1)}, u32[]{:S(2)}, u32[]{:S(2)}) %collective-permute-start.7) | collective-permute-done | bytes 131104 | tf_op jit(solution)/shard_map/ppermute | solution.py:20
  30.8 0.7 %pad_maximum_fusion.phase = f32[256,256]{1,0:T(8,128)} fusion(f32[256,128]{1,0:T(8,128)S(1)} %collective-permute-done.7, f32[256,128]{1,0:T(8,128)S(1)} %constant_dynamic-update-slice_fusion), kind=kLoop, calls=%fused_computation | loop fusion | flops 65536 | bytes 524288 | tf_op jit(solution)/shard_map/concatenate | solution.py:304
  31.5 2.1 %transmission.1.refs_4_ = f32[2,128,256]{2,1,0:T(8,128)} custom-call(f32[256,256]{1,0:T(8,128)} %pad_maximum_fusion.phase, f32[8,8,128]{2,1,0:T(8,128)} %slot_parameters.1.refs_5_.params), custom_call_target="tpu_custom_call" | custom-call | tf_op jit(solution)/shard_map/transmission/pallas_call | solution.py:248
  33.7 12.9 %collective-permute-done.4.refs_2_ = f32[2,128,256]{2,1,0:T(8,128)S(1)} collective-permute-done((f32[2,128,256]{2,1,0:T(8,128)}, f32[2,128,256]{2,1,0:T(8,128)S(1)}, u32[]{:S(2)}, u32[]{:S(2)}) %collective-permute-start.4) | collective-permute-done | bytes 262176 | tf_op jit(solution)/shard_map/ppermute | solution.py:20
  46.6 1.9 %collective-permute-done.5.refs_3_ = f32[2,128,256]{2,1,0:T(8,128)S(1)} collective-permute-done((f32[2,128,256]{2,1,0:T(8,128)}, f32[2,128,256]{2,1,0:T(8,128)S(1)}, u32[]{:S(2)}, u32[]{:S(2)}) %collective-permute-start.5) | collective-permute-done | bytes 262176 | tf_op jit(solution)/shard_map/ppermute | solution.py:20
  48.5 0.7 %copy-done.5 = f32[2,128,256]{2,1,0:T(8,128)} copy-done((f32[2,128,256]{2,1,0:T(8,128)}, f32[2,128,256]{2,1,0:T(8,128)S(1)}, u32[]{:S(2)}) %copy-start.5) | copy-done | bytes 262168
  49.2 2.8 %patterns.1 = f32[1,1,2,128,128]{4,3,2,1,0:T(8,128)} custom-call(f32[2,128,256]{2,1,0:T(8,128)} %get-tuple-element.17.refs_0_, f32[2,128,256]{2,1,0:T(8,128)} %copy-done.1, f32[2,128,256]{2,1,0:T(8,128)} %copy-done.3, f32[2,128,256]{2,1,0:T(8,128)} %copy-done.5, f32[2,128,256]{2,1,0:T(8,128)} %transmission.1.refs_4_, ...), custom_call_target="tpu_custom_call" | custom-call | flops 201326592 | bytes 2097152 | tf_op jit(solution)/shard_map/patterns/pallas_call | solution.py:248
  (26 shorter events, 0.8 us)
Async XLA Ops:
  0.0 5.8 %copy-start.6 = (f32[128,128]{1,0:T(8,128)S(1)}, f32[128,128]{1,0:T(8,128)}, u32[]{:S(2)}) copy-start(f32[128,128]{1,0:T(8,128)} %param.17) | copy-start | bytes 196612
  3.6 7.6 %collective-permute-start = (f32[2,2,128,128]{3,2,1,0:T(8,128)}, f32[2,2,128,128]{3,2,1,0:T(8,128)S(1)}, u32[]{:S(2)}, u32[]{:S(2)}) collective-permute-start(f32[2,2,128,128]{3,2,1,0:T(8,128)} %get-tuple-element.14), channel_id=1, source_target_pairs={{0,4},{4,8},{8,12},{12,0},{1,5},{5,9},{9,13},{13,1},{2,6},{6,10},{... | collective-permute-start | bytes 786440 | tf_op jit(solution)/shard_map/ppermute | solution.py:20
  5.4 12.1 %collective-permute-start.1 = (f32[2,2,128,128]{3,2,1,0:T(8,128)}, f32[2,2,128,128]{3,2,1,0:T(8,128)S(1)}, u32[]{:S(2)}, u32[]{:S(2)}) collective-permute-start(f32[2,2,128,128]{3,2,1,0:T(8,128)} %get-tuple-element.15), channel_id=1, source_target_pairs={{0,8},{4,12},{8,0},{12,4},{1,9},{5,13},{9,1},{13,5},{2,10},{6,14},... | collective-permute-start | bytes 786440 | tf_op jit(solution)/shard_map/ppermute | solution.py:20
  5.6 0.7 %copy-start.8 = (s32[16,2]{0,1:T(2,128)S(1)}, s32[16,2]{0,1:T(2,128)}, u32[]{:S(2)}) copy-start(s32[16,2]{0,1:T(2,128)} %param.21) | copy-start | bytes 388
  5.6 12.4 %collective-permute-start.2 = (f32[2,2,128,128]{3,2,1,0:T(8,128)}, f32[2,2,128,128]{3,2,1,0:T(8,128)S(1)}, u32[]{:S(2)}, u32[]{:S(2)}) collective-permute-start(f32[2,2,128,128]{3,2,1,0:T(8,128)} %get-tuple-element.16), channel_id=1, source_target_pairs={{0,12},{4,0},{8,4},{12,8},{1,13},{5,1},{9,5},{13,9},{2,14},{6,2},{... | collective-permute-start | bytes 786440 | tf_op jit(solution)/shard_map/ppermute | solution.py:20
  5.8 20.3 %collective-permute-start.6 = (f32[128,128]{1,0:T(8,128)S(1)}, f32[128,128]{1,0:T(8,128)S(1)}, u32[]{:S(2)}, u32[]{:S(2)}) collective-permute-start(f32[128,128]{1,0:T(8,128)S(1)} %copy-done.6), channel_id=1, source_target_pairs={{0,3},{1,0},{2,1},{3,2},{4,7},{5,4},{6,5},{7,6},{8,11},{9,8},{10,9... | collective-permute-start | bytes 196616 | tf_op jit(solution)/shard_map/ppermute | solution.py:20
  6.4 0.7 %copy-start.7 = (s32[4,4,2]{1,2,0:T(2,128)S(1)}, s32[4,4,2]{1,2,0:T(2,128)}, u32[]{:S(2)}) copy-start(s32[4,4,2]{1,2,0:T(2,128)} %param.22) | copy-start | bytes 388
  7.2 0.7 %copy-start.9 = (s32[4,2]{0,1:T(2,128)S(1)}, s32[4,2]{0,1:T(2,128)}, u32[]{:S(2)}) copy-start(s32[4,2]{0,1:T(2,128)} %param.20) | copy-start | bytes 100
  11.2 6.8 %copy-start = (f32[2,2,128,128]{3,2,1,0:T(8,128)}, f32[2,2,128,128]{3,2,1,0:T(8,128)S(1)}, u32[]{:S(2)}) copy-start(f32[2,2,128,128]{3,2,1,0:T(8,128)S(1)} %collective-permute-done.refs_1_) | copy-start | bytes 786436
  17.4 0.7 %copy-start.2 = (f32[2,2,128,128]{3,2,1,0:T(8,128)}, f32[2,2,128,128]{3,2,1,0:T(8,128)S(1)}, u32[]{:S(2)}) copy-start(f32[2,2,128,128]{3,2,1,0:T(8,128)S(1)} %collective-permute-done.1.refs_2_) | copy-start | bytes 786436
  18.0 0.7 %copy-start.4 = (f32[2,2,128,128]{3,2,1,0:T(8,128)}, f32[2,2,128,128]{3,2,1,0:T(8,128)S(1)}, u32[]{:S(2)}) copy-start(f32[2,2,128,128]{3,2,1,0:T(8,128)S(1)} %collective-permute-done.2.refs_3_) | copy-start | bytes 786436
  22.3 11.4 %collective-permute-start.3 = (f32[2,128,256]{2,1,0:T(8,128)}, f32[2,128,256]{2,1,0:T(8,128)S(1)}, u32[]{:S(2)}, u32[]{:S(2)}) collective-permute-start(f32[2,128,256]{2,1,0:T(8,128)} %get-tuple-element.18), channel_id=1, source_target_pairs={{0,1},{1,2},{2,3},{3,0},{4,5},{5,6},{6,7},{7,4},{8,9},{9,10},{10,1... | collective-permute-start | bytes 786440 | tf_op jit(solution)/shard_map/ppermute | solution.py:20
  23.5 23.0 %collective-permute-start.4 = (f32[2,128,256]{2,1,0:T(8,128)}, f32[2,128,256]{2,1,0:T(8,128)S(1)}, u32[]{:S(2)}, u32[]{:S(2)}) collective-permute-start(f32[2,128,256]{2,1,0:T(8,128)} %get-tuple-element.19), channel_id=1, source_target_pairs={{0,2},{1,3},{2,0},{3,1},{4,6},{5,7},{6,4},{7,5},{8,10},{9,11},{10,... | collective-permute-start | bytes 786440 | tf_op jit(solution)/shard_map/ppermute | solution.py:20
  24.6 23.9 %collective-permute-start.5 = (f32[2,128,256]{2,1,0:T(8,128)}, f32[2,128,256]{2,1,0:T(8,128)S(1)}, u32[]{:S(2)}, u32[]{:S(2)}) collective-permute-start(f32[2,128,256]{2,1,0:T(8,128)} %get-tuple-element.20), channel_id=1, source_target_pairs={{0,3},{1,0},{2,1},{3,2},{4,7},{5,4},{6,5},{7,6},{8,11},{9,8},{10,9... | collective-permute-start | bytes 786440 | tf_op jit(solution)/shard_map/ppermute | solution.py:20
  26.1 4.7 %collective-permute-start.7 = (f32[256,128]{1,0:T(8,128)S(1)}, f32[256,128]{1,0:T(8,128)S(1)}, u32[]{:S(2)}, u32[]{:S(2)}) collective-permute-start(f32[256,128]{1,0:T(8,128)S(1)} %constant_dynamic-update-slice_fusion), channel_id=1, source_target_pairs={{0,12},{4,0},{8,4},{12,8},{1,13},{5,1},{9,5},{13,9},{2,14},{6,2},{... | collective-permute-start | bytes 393224 | tf_op jit(solution)/shard_map/ppermute | solution.py:20
  33.7 14.8 %copy-start.1 = (f32[2,128,256]{2,1,0:T(8,128)}, f32[2,128,256]{2,1,0:T(8,128)S(1)}, u32[]{:S(2)}) copy-start(f32[2,128,256]{2,1,0:T(8,128)S(1)} %collective-permute-done.3.refs_1_) | copy-start | bytes 786436
  46.6 1.9 %copy-start.3 = (f32[2,128,256]{2,1,0:T(8,128)}, f32[2,128,256]{2,1,0:T(8,128)S(1)}, u32[]{:S(2)}) copy-start(f32[2,128,256]{2,1,0:T(8,128)S(1)} %collective-permute-done.4.refs_2_) | copy-start | bytes 786436
  48.5 0.7 %copy-start.5 = (f32[2,128,256]{2,1,0:T(8,128)}, f32[2,128,256]{2,1,0:T(8,128)S(1)}, u32[]{:S(2)}) copy-start(f32[2,128,256]{2,1,0:T(8,128)S(1)} %collective-permute-done.5.refs_3_) | copy-start | bytes 786436
where the time goes:
time: 52.3 us; the launch traced here: 52 us
  waiting for transfers between devices  26.9 us (51%)
  Pallas kernels  13.5 us (26%)
  starting transfers between devices  6.81 us (13%)
  local copies, waits for them, and re-layouts  4.01 us (8%)
  other arithmetic  0.74 us (1%)
    ppermute x8, waiting for transfers between devices, shift(): lax.ppermute(shard, axis, [(i, (i + by) % devices) for i in range(devices)])  26.9 us
    pallas_call x5, Pallas kernels, call(): pl.pallas_call(kernel, name=name, out_shape=outs, in_specs=[scalar if at...  13.5 us
    ppermute x8, starting transfers between devices, shift(): lax.ppermute(shard, axis, [(i, (i + by) % devices) for i in range(devices)])  6.81 us
    unnamed x24, local copies, waits for them, and re-layouts  2.14 us
  transfers between devices with their start and end apart: 8, of which 6 were waited for; matrix products, arithmetic and copies ran while one was open for 6% of the time, Pallas kernels for 14%

commit v1 on v0

v1 whole, which is shorter than its diff:
```python
import functools
import math

import jax
import jax.numpy as jnp
import numpy as np
from jax import lax
from jax.experimental import pallas as pl
from jax.experimental.pallas import tpu as pltpu
from jax.sharding import PartitionSpec as P

WIN = 128
CHUNKS = 2
HALF = WIN // CHUNKS
LANES = 2 * HALF

prop_coef = 3e-05
f32, bf16 = jnp.float32, jnp.bfloat16


def shift(shard, axis, by):
    devices = lax.axis_size(axis)
    return lax.ppermute(shard, axis, [(i, (i + by) % devices) for i in range(devices)])


def split_table(table):
    high = np.asarray(table, np.float32).astype(bf16)
    low = (np.asarray(table, np.float64) - high.astype(np.float64)).astype(np.float32).astype(bf16)
    return high, low


def wave_table(length):
    index = np.arange(length)
    freq = np.where(index < length // 2, index, index - length).astype(np.float64)
    turns = (index[:, None] * index[None, :]) % length
    angle = 2.0 * math.pi / length * turns - prop_coef * (freq * freq)[:, None]
    return np.cos(angle) / math.sqrt(length), np.sin(angle) / math.sqrt(length)


def row_tables(length, tile_cols, tiles):
    real, imag = wave_table(length)
    cols = (np.arange(tiles)[:, None] * tile_cols + np.arange(WIN)[None, :]) % length
    cols = cols.reshape(tiles, CHUNKS, HALF)
    both = np.concatenate([real[:, cols], imag[:, cols]], axis=3)
    return split_table(np.transpose(both, (2, 1, 0, 3)))


def column_tables(length):
    radix = length // WIN
    real, imag = wave_table(length)
    parts = []
    for k0 in range(radix):
        both = np.concatenate([real[k0::radix, :WIN].T, imag[k0::radix, :WIN].T], axis=0)
        high, low = split_table(both)
        parts.append(np.concatenate([high, low, high], axis=1))
    return np.stack(parts)


def window_tables():
    index = np.arange(WIN)
    angle = -2.0 * math.pi / WIN * ((index[:, None] * index[None, :]) % WIN)
    real, imag = np.cos(angle) / math.sqrt(WIN), np.sin(angle) / math.sqrt(WIN)
    left = np.concatenate([real, imag], axis=1)
    rows = []
    for chunk in range(CHUNKS):
        at = slice(chunk * HALF, (chunk + 1) * HALF)
        rows += [np.concatenate([real[at], imag[at]], 1), np.concatenate([-imag[at], real[at]], 1)]
    return split_table(left) + split_table(np.concatenate(rows, axis=0))


def split(value):
    high = value.astype(bf16)
    return high, (value - high.astype(f32)).astype(bf16)


def mul(left, right):
    return jnp.dot(left, right, preferred_element_type=f32)


def signs(rows):
    lane = lax.broadcasted_iota(jnp.int32, (rows, LANES), 1)
    return jnp.where(lane < HALF, -1.0, 1.0).astype(f32)


def swap(value):
    return pltpu.roll(value, HALF, 1)


def row_kernel(tiles, step, spectra, high, low, *messages):
    me = lax.axis_index("row")
    rows = spectra.shape[2]
    sign = signs(rows)
    lhs_high, lhs_low = split(jnp.concatenate([spectra[0, 0], spectra[1, 0]], axis=0))
    for k in range(0, tiles, 2):
        pair = [lax.rem(me + k + n, tiles) for n in range(2)]
        table = jnp.concatenate([high[0, tile] for tile in pair], axis=1)
        small = jnp.concatenate([low[0, tile] for tile in pair], axis=1)
        both = mul(lhs_high, table) + mul(lhs_low, table) + mul(lhs_high, small)
        for n in range(2):
            piece = both[:, n * LANES : (n + 1) * LANES]
            wave = piece[:rows] + sign * swap(piece[rows:])
            for block, to in enumerate((k + n, (k + n - step) % tiles)):
                messages[to][block] = wave


def prep_kernel(sizes, slots_ref, corners, freq, amp_re, amp_im, cosine, sine, params):
    row_tiles, col_tiles, slots, probes, tile_rows, tile_cols, grid_len = sizes
    beam_pos, row_pos = lax.axis_index("beam"), lax.axis_index("row")
    for k in range(row_tiles):
        tile = target(k, beam_pos, row_tiles)
        for s in range(slots):
            probe = slots_ref[(tile * col_tiles + row_pos) * slots + s]
            live = (probe < probes).astype(f32)
            safe = jnp.minimum(probe, probes - 1)
            top, left = corners[2 * safe], corners[2 * safe + 1]
            turns = lax.rem(top * freq[2 * beam_pos] + left * freq[2 * beam_pos + 1], grid_len)
            turns = lax.rem(turns + grid_len, grid_len)
            re, im = amp_re[beam_pos] * live, amp_im[beam_pos] * live
            c, n = cosine[turns], sine[turns]
            values = [
                re * c - im * n,
                re * n + im * c,
                jnp.clip(top - tile * tile_rows, 0, tile_rows - 1).astype(f32),
                jnp.clip(left - row_pos * tile_cols, 0, tile_cols - 1).astype(f32),
            ]
            for at, value in enumerate(values):
                params[k * slots + s, at] = jnp.full((LANES,), value, f32)


def masks_of(params, at, chunk):
    row = lax.broadcasted_iota(jnp.int32, (WIN, LANES), 0).astype(f32)
    lane = lax.broadcasted_iota(jnp.int32, (WIN, LANES), 1)
    col = (jnp.where(lane < HALF, lane, lane - HALF) + chunk * HALF).astype(f32)
    return row >= params[at, 2:3, :], col >= params[at, 3:4, :]


def pick(rows_here, cols_here, near_near, near_far, far_near, far_far):
    return jnp.where(
        rows_here,
        jnp.where(cols_here, near_near, near_far),
        jnp.where(cols_here, far_near, far_far),
    )


def transmit_kernel(slots, phase, params, out):
    sign = signs(WIN)
    for chunk in range(CHUNKS):
        at = slice(chunk * HALF, (chunk + 1) * HALF)
        after = slice(WIN + chunk * HALF, WIN + (chunk + 1) * HALF)
        blocks = [
            jnp.concatenate([phase[rows, cols]] * 2, axis=1)
            for rows in (slice(0, WIN), slice(WIN, 2 * WIN))
            for cols in (at, after)
        ]
        for s in range(slots):
            value = pick(*masks_of(params, s, chunk), *blocks)
            out[chunk, s, 0] = jnp.cos(value)
            out[chunk, s, 1] = jnp.sin(value) * sign


def column_kernel(sizes, chunk, *refs):
    sources, radix, row_tiles, slots, tile_rows = sizes
    arrived, (table, params) = refs[:sources], refs[sources : sources + 2]
    sends = refs[sources + 2 : sources + 2 + row_tiles]
    gathered, waves = refs[sources + 2 + row_tiles :]
    row_pos, beam_pos = lax.axis_index("row"), lax.axis_index("beam")
    part = arrived[0].shape[1] // radix
    grid_len = radix * WIN
    sign = signs(WIN)
    for k in range(sources):
        source = lax.rem(row_pos + sources - k, sources)
        at = pl.ds(pl.multiple_of(source * part, part), part)
        for k0 in range(radix):
            for block in range(2):
                gathered[k0, at, block * LANES : (block + 1) * LANES] = arrived[k][
                    block, pl.ds(k0, part, stride=radix), :
                ]
    pieces = []
    for k0 in range(radix):
        high, low = split(gathered[k0])
        both = mul(table[k0], jnp.concatenate([high, high, low], axis=0))
        halves = []
        for block in range(2):
            piece = both[:, block * LANES : (block + 1) * LANES]
            halves.append(piece[:WIN] + sign * swap(piece[WIN:]))
        pieces.append(halves)
    for block in range(2):
        at = slice(block * LANES, (block + 1) * LANES)
        zero, one, two, three = (pieces[k0][block] for k0 in range(radix))
        even, odd = zero + two, one + three
        even_turned, odd_turned = zero - two, sign * swap(one - three)
        rows = [even + odd, even_turned + odd_turned, even - odd, even_turned - odd_turned]
        for a in range(radix + 1):
            waves[a * WIN : (a + 1) * WIN, at] = rows[a % radix]
    for k in range(row_tiles):
        start = target(k, beam_pos, row_tiles) * tile_rows
        near = pl.ds(pl.multiple_of(start, 8), WIN)
        far = pl.ds(pl.multiple_of(lax.rem(start + WIN, grid_len), 8), WIN)
        for s in range(slots):
            which = k * slots + s
            first, second = slice(0, LANES), slice(LANES, 2 * LANES)
            wave = pick(
                *masks_of(params, which, chunk),
                waves[near, first],
                waves[near, second],
                waves[far, first],
                waves[far, second],
            )
            coef_re, coef_im = params[which, 0:1, :], params[which, 1:2, :]
            sends[k][s] = wave * coef_re + (sign * coef_im) * swap(wave)


def pattern_kernel(slots, *refs):
    transmit, left_high, left_low, right_high, right_low, out = refs[-6:]
    arrived = refs[:-6]
    each = len(arrived) // CHUNKS
    sign = signs(WIN)
    values, turned = [], []
    for s in range(slots):
        for chunk in range(CHUNKS):
            wave = arrived[chunk * each][s]
            for part in arrived[chunk * each + 1 : (chunk + 1) * each]:
                wave = wave + part[s]
            wave = wave * transmit[chunk, s, 0] + swap(wave) * transmit[chunk, s, 1]
            values.append(wave)
            turned.append(sign * swap(wave))
    window = jnp.concatenate(
        [jnp.concatenate(values, axis=1), jnp.concatenate(turned, axis=1)], axis=0
    )
    high, low = split(window)
    inner = mul(left_high[...], high) + mul(left_high[...], low) + mul(left_low[...], high)
    inner = jnp.concatenate(
        [inner[:, s * 2 * WIN : (s + 1) * 2 * WIN] for s in range(slots)], axis=0
    )
    high, low = split(inner)
    outer = mul(high, right_high[...]) + mul(low, right_high[...]) + mul(high, right_low[...])
    power = outer[:, :WIN] * outer[:, :WIN] + outer[:, WIN:] * outer[:, WIN:]
    for s in range(slots):
        out[0, 0, s] = power[s * WIN : (s + 1) * WIN]


def on_line(devices):
    return devices == 4


def target(k, beam_pos, devices):
    if not on_line(devices):
        return lax.rem(beam_pos + k, devices)
    first = jnp.where(beam_pos % 2 == 0, 3, 0)
    second = jnp.where(beam_pos < 2, 2, 1)
    return [beam_pos, first, second, 6 - beam_pos - first - second][k]


def sum_over_beams(sends):
    devices = len(sends)
    if not on_line(devices):
        return [sends[0]] + [shift(sends[k], "beam", k) for k in range(1, devices)]
    own, first, second, third = sends
    beam_pos = lax.axis_index("beam")
    inside = (beam_pos == 1) | (beam_pos == 2)
    one = lax.ppermute(first, "beam", [(0, 1), (1, 0), (2, 3), (3, 2)])
    two = lax.ppermute(second, "beam", [(1, 2), (2, 1)])
    three = lax.ppermute(second, "beam", [(0, 2), (3, 1)])
    relayed = jnp.where(inside, third + one, third)
    four = lax.ppermute(relayed, "beam", [(0, 1), (1, 3), (2, 0), (3, 2)])
    return [own + jnp.where(inside, two, one), three, four]


def call(kernel, name, ins, outs, smem=(), scratch=(), flops=0, moved=0):
    vmem, scalar = pl.BlockSpec(memory_space=pltpu.VMEM), pl.BlockSpec(memory_space=pltpu.SMEM)
    return pl.pallas_call(
        kernel,
        name=name,
        out_shape=outs,
        in_specs=[scalar if at in smem else vmem for at in range(len(ins))],
        out_specs=jax.tree.map(lambda _: vmem, outs),
        scratch_shapes=list(scratch),
        cost_estimate=pl.CostEstimate(flops=flops, bytes_accessed=moved, transcendentals=0),
    )(*ins)


def local(spectra, potential, amp_re, amp_im, beam_freq, probe_corners, slot_table):
    ky_rows, grid_len = spectra.shape[2], spectra.shape[3]
    tile_rows, tile_cols = potential.shape
    row_tiles, col_tiles, slots = slot_table.shape
    probes = probe_corners.shape[0]
    radix = grid_len // WIN

    def floats(*shape):
        return jax.ShapeDtypeStruct(shape, f32)

    row_high, row_low = row_tables(grid_len, tile_cols, col_tiles)
    arrived = []
    for chunk in range(CHUNKS):
        messages = call(
            functools.partial(row_kernel, col_tiles, WIN // tile_cols),
            f"row_transform_{chunk}",
            (
                spectra,
                jnp.asarray(row_high[chunk : chunk + 1]),
                jnp.asarray(row_low[chunk : chunk + 1]),
            ),
            [floats(2, ky_rows, LANES)] * col_tiles,
            flops=24 * ky_rows * grid_len * HALF * col_tiles,
            moved=4 << 20,
        )
        order = sorted(range(1, col_tiles), key=lambda k: -min(k, col_tiles - k))
        moved = {k: shift(messages[k], "row", k) for k in order}
        arrived.append([messages[0]] + [moved[k] for k in range(1, col_tiles)])

    index = np.arange(grid_len)
    angle = -2.0 * math.pi / grid_len * index
    params = call(
        functools.partial(
            prep_kernel,
            (row_tiles, col_tiles, slots, probes, tile_rows, tile_cols, grid_len),
        ),
        "slot_parameters",
        (
            slot_table.reshape(-1),
            probe_corners.reshape(-1),
            beam_freq.reshape(-1),
            amp_re,
            amp_im,
            jnp.asarray(np.cos(angle), f32),
            jnp.asarray(np.sin(angle), f32),
        ),
        floats(row_tiles * slots, 8, LANES),
        smem=range(7),
    )

    below = [potential] + [shift(potential, "beam", -k) for k in range(1, WIN // tile_rows + 1)]
    tall = jnp.concatenate(below, axis=0)
    beside = [tall] + [shift(tall, "row", -k) for k in range(1, WIN // tile_cols + 1)]
    phase = jnp.concatenate(beside, axis=1)
    phase = jnp.pad(phase, [(0, 2 * WIN - length) for length in phase.shape])
    transmit = call(
        functools.partial(transmit_kernel, slots),
        "transmission",
        (phase, params),
        floats(CHUNKS, slots, 2, WIN, LANES),
    )

    table = jnp.asarray(column_tables(grid_len))
    parts = []
    for chunk in range(CHUNKS):
        sends = call(
            functools.partial(
                column_kernel, (col_tiles, radix, row_tiles, slots, tile_rows), chunk
            ),
            f"column_transform_{chunk}",
            (*arrived[chunk], table, params),
            [floats(slots, WIN, LANES)] * row_tiles,
            scratch=(
                pltpu.VMEM((radix, WIN, 2 * LANES), f32),
                pltpu.VMEM((grid_len + WIN, 2 * LANES), f32),
            ),
            flops=24 * grid_len * WIN * 2 * HALF,
            moved=2 << 20,
        )
        parts += sum_over_beams(sends)

    return call(
        functools.partial(pattern_kernel, slots),
        "patterns",
        (*parts, transmit, *(jnp.asarray(table) for table in window_tables())),
        floats(1, 1, slots, WIN, WIN),
        flops=48 * slots * WIN * WIN * WIN,
        moved=2 << 20,
    )


def solution(mesh):
    return jax.shard_map(
        local,
        mesh=mesh,
        in_specs=(
            P(None, ("phonon", "beam"), "row", None),
            P(("phonon", "beam"), "row"),
            P(),
            P(),
            P(),
            P(),
            P(),
        ),
        out_specs=P(("phonon", "beam"), "row", None, None, None),
        check_vma=False,
    )
```

time: 52.3 us -> 55.7 us (1.065)
  the two profiles are of different devices: /device:TPU:9 before, /device:TPU:0 now
where the time goes in v1:
time: 55.7 us; the launch traced here: 55.3 us
  starting transfers between devices  22.6 us (41%)
  Pallas kernels  18.9 us (34%)
  waiting for transfers between devices  6.61 us (12%)
  local copies, waits for them, and re-layouts  4.85 us (9%)
  other arithmetic  2.09 us (4%)
    pallas_call x7, Pallas kernels, call(): pl.pallas_call(kernel, name=name, out_shape=outs, in_specs=[scalar if at...  18.9 us
    ppermute x8, starting transfers between devices, shift(): lax.ppermute(shard, axis, [(i, (i + by) % devices) for i in range(devices)])  9.85 us
    ppermute x2, starting transfers between devices, sum_over_beams(): three = lax.ppermute(second, 'beam', [(0, 2), (3, 1)])  6.84 us
    ppermute x2, waiting for transfers between devices, sum_over_beams(): one = lax.ppermute(first, 'beam', [(0, 1), (1, 0), (2, 3), (3, 2)])  5.44 us
    ppermute x2, starting transfers between devices, sum_over_beams(): four = lax.ppermute(relayed, 'beam', [(0, 1), (1, 3), (2, 0), (3, 2)])  3.11 us
    unnamed x44, local copies, waits for them, and re-layouts  2.99 us
    ppermute x2, starting transfers between devices, sum_over_beams(): two = lax.ppermute(second, 'beam', [(1, 2), (2, 1)])  1.45 us
    ppermute x2, starting transfers between devices, sum_over_beams(): one = lax.ppermute(first, 'beam', [(0, 1), (1, 0), (2, 3), (3, 2)])  1.39 us
  transfers between devices with their start and end apart: 16, of which 2 were waited for; matrix products, arithmetic and copies ran while one was open for 8% of the time, Pallas kernels for 24%

profile of v1, /device:TPU:0, one launch (start us, length us, event | category | flops | bytes accessed | tf_op | source)
XLA Modules:
  0.0 55.3 jit_solution(12041713133339311392)
XLA Ops:
  0.0 2.9 %row_transform_1.1 = (f32[2,128,128]{2,1,0:T(8,128)}, f32[2,128,128]{2,1,0:T(8,128)}, f32[2,128,128]{2,1,0:T(8,128)}, f32[2,128,128]{2,1,0:T(8,128)}) custom-call(f32[2,1,128,512]{3,2,1,0:T(8,128)} %spectra.3, bf16[1,4,512,128]{3,2,1,0:T(8,128)(2,1)} %constant.33.clone.high, bf16[1,4,512,128]{3,2,1,0:T(8,128)(2,1)} %constant.34.clone.low), custom_call_target="tpu_custom_call" | custom-call | flops 402653184 | bytes 4194304 | tf_op jit(solution)/shard_map/row_transform_1/pallas_call | solution.py:271
  3.3 2.5 %collective-permute-start.8 = (f32[2,128,128]{2,1,0:T(8,128)}, f32[2,128,128]{2,1,0:T(8,128)S(1)}, u32[]{:S(2)}, u32[]{:S(2)}) collective-permute-start(f32[2,128,128]{2,1,0:T(8,128)} %get-tuple-element.31), channel_id=1, source_target_pairs={{0,8},{4,12},{8,0},{12,4},{1,9},{5,13},{9,1},{13,5},{2,10},{6,14},... | collective-permute-start | bytes 393224 | tf_op jit(solution)/shard_map/ppermute | solution.py:23
  5.8 1.5 %collective-permute-start.9 = (f32[2,128,128]{2,1,0:T(8,128)}, f32[2,128,128]{2,1,0:T(8,128)S(1)}, u32[]{:S(2)}, u32[]{:S(2)}) collective-permute-start(f32[2,128,128]{2,1,0:T(8,128)} %get-tuple-element.32), channel_id=1, source_target_pairs={{0,12},{4,0},{8,4},{12,8},{1,13},{5,1},{9,5},{13,9},{2,14},{6,2},{... | collective-permute-start | bytes 393224 | tf_op jit(solution)/shard_map/ppermute | solution.py:23
  7.3 2.8 %row_transform_0.1 = (f32[2,128,128]{2,1,0:T(8,128)}, f32[2,128,128]{2,1,0:T(8,128)}, f32[2,128,128]{2,1,0:T(8,128)}, f32[2,128,128]{2,1,0:T(8,128)}) custom-call(f32[2,1,128,512]{3,2,1,0:T(8,128)} %spectra.3, bf16[1,4,512,128]{3,2,1,0:T(8,128)(2,1)} %constant.13.clone.high, bf16[1,4,512,128]{3,2,1,0:T(8,128)(2,1)} %constant.32.clone.low), custom_call_target="tpu_custom_call" | custom-call | flops 402653184 | bytes 4194304 | tf_op jit(solution)/shard_map/row_transform_0/pallas_call | solution.py:271
  10.1 3.7 %collective-permute-start.14 = (f32[128,128]{1,0:T(8,128)S(1)}, f32[128,128]{1,0:T(8,128)S(1)}, u32[]{:S(2)}, u32[]{:S(2)}) collective-permute-start(f32[128,128]{1,0:T(8,128)S(1)} %copy-done.14), channel_id=1, source_target_pairs={{0,3},{1,0},{2,1},{3,2},{4,7},{5,4},{6,5},{7,6},{8,11},{9,8},{10,9... | collective-permute-start | bytes 196616 | tf_op jit(solution)/shard_map/ppermute | solution.py:23
  13.8 0.7 %copy-done.16 = s32[16,2]{0,1:T(2,128)S(1)} copy-done((s32[16,2]{0,1:T(2,128)S(1)}, s32[16,2]{0,1:T(2,128)}, u32[]{:S(2)}) %copy-start.16) | copy-done | bytes 152
  14.6 0.7 %reshape.10.corners = s32[32]{0:T(128)} reshape(s32[16,2]{1,0:T(8,128)S(1)} %copy.23) | data formatting | bytes 256 | tf_op jit(solution)/shard_map/reshape | solution.py:321
  16.7 1.5 %slot_parameters.1.refs_5_.params = f32[8,8,128]{2,1,0:T(8,128)} custom-call(s32[32]{0:T(128)} %reshape.9.slots_ref, s32[32]{0:T(128)} %reshape.10.corners, s32[8]{0:T(128)} %reshape.11.freq, f32[4]{0:T(128)} %amp_re.1, f32[4]{0:T(128)} %amp_im.1, f32[512]{0:T(512)} %constant.35.clone.cosine, f32[512]{0:T(512)} %constant.36.clone.sine), custom_call_target="tpu_custom_call" | custom-call | tf_op jit(solution)/shard_map/slot_parameters/pallas_call | solution.py:271
  18.8 1.2 %collective-permute-start.2 = (f32[2,128,128]{2,1,0:T(8,128)S(1)}, f32[2,128,128]{2,1,0:T(8,128)S(1)}, u32[]{:S(2)}, u32[]{:S(2)}) collective-permute-start(f32[2,128,128]{2,1,0:T(8,128)S(1)} %copy-done.19), channel_id=1, source_target_pairs={{0,12},{4,0},{8,4},{12,8},{1,13},{5,1},{9,5},{13,9},{2,14},{6,2},{... | collective-permute-start | bytes 393224 | tf_op jit(solution)/shard_map/ppermute | solution.py:23
  20.6 3.0 %column_transform_1.1 = (f32[2,128,128]{2,1,0:T(8,128)}, f32[2,128,128]{2,1,0:T(8,128)}, f32[2,128,128]{2,1,0:T(8,128)}, f32[2,128,128]{2,1,0:T(8,128)}) custom-call(f32[2,128,128]{2,1,0:T(8,128)} %get-tuple-element.29.refs_0_, f32[2,128,128]{2,1,0:T(8,128)} %copy-done.9, f32[2,128,128]{2,1,0:T(8,128)} %copy-done.10, f32[2,128,128]{2,1,0:T(8,128)} %copy-done.11, ...), custom_call_target="tpu_custom_call" | custom-call | flops 201326592 | bytes 2097152 | tf_op jit(solution)/shard_map/column_transform_1/pallas_call | solution.py:271
  23.6 0.8 %collective-permute-start.10 = (f32[2,128,128]{2,1,0:T(8,128)}, f32[2,128,128]{2,1,0:T(8,128)S(1)}, u32[]{:S(2)}, u32[]{:S(2)}) collective-permute-start(f32[2,128,128]{2,1,0:T(8,128)} %get-tuple-element.34), channel_id=1, source_target_pairs={{1,2},{2,1},{5,6},{6,5},{9,10},{10,9},{13,14},{14,13},{17,18},{18,... | collective-permute-start | bytes 393224 | tf_op jit(solution)/shard_map/ppermute | solution.py:262
  24.4 1.3 %collective-permute-start.11 = (f32[2,128,128]{2,1,0:T(8,128)}, f32[2,128,128]{2,1,0:T(8,128)S(1)}, u32[]{:S(2)}, u32[]{:S(2)}) collective-permute-start(f32[2,128,128]{2,1,0:T(8,128)} %get-tuple-element.35), channel_id=1, source_target_pairs={{0,1},{1,0},{2,3},{3,2},{4,5},{5,4},{6,7},{7,6},{8,9},{9,8},{10,11... | collective-permute-start | bytes 393224 | tf_op jit(solution)/shard_map/ppermute | solution.py:261
  25.8 2.0 %collective-permute-start.12 = (f32[2,128,128]{2,1,0:T(8,128)S(1)}, f32[2,128,128]{2,1,0:T(8,128)S(1)}, u32[]{:S(2)}, u32[]{:S(2)}) collective-permute-start(f32[2,128,128]{2,1,0:T(8,128)S(1)} %copy-done.18), channel_id=1, source_target_pairs={{0,2},{3,1},{4,6},{7,5},{8,10},{11,9},{12,14},{15,13},{16,18},{19,... | collective-permute-start | bytes 393224 | tf_op jit(solution)/shard_map/ppermute | solution.py:263
  28.5 3.0 %column_transform_0.1 = (f32[2,128,128]{2,1,0:T(8,128)}, f32[2,128,128]{2,1,0:T(8,128)}, f32[2,128,128]{2,1,0:T(8,128)}, f32[2,128,128]{2,1,0:T(8,128)}) custom-call(f32[2,128,128]{2,1,0:T(8,128)} %get-tuple-element.21.refs_0_, f32[2,128,128]{2,1,0:T(8,128)} %copy-done.8, f32[2,128,128]{2,1,0:T(8,128)} %copy-done.12, f32[2,128,128]{2,1,0:T(8,128)} %copy-done.13, ...), custom_call_target="tpu_custom_call" | custom-call | flops 201326592 | bytes 2097152 | tf_op jit(solution)/shard_map/column_transform_0/pallas_call | solution.py:271
  32.1 4.9 %collective-permute-start.5 = (f32[2,128,128]{2,1,0:T(8,128)}, f32[2,128,128]{2,1,0:T(8,128)S(1)}, u32[]{:S(2)}, u32[]{:S(2)}) collective-permute-start(f32[2,128,128]{2,1,0:T(8,128)} %get-tuple-element.26), channel_id=1, source_target_pairs={{0,2},{3,1},{4,6},{7,5},{8,10},{11,9},{12,14},{15,13},{16,18},{19,... | collective-permute-start | bytes 393224 | tf_op jit(solution)/shard_map/ppermute | solution.py:263
  37.1 0.7 %add_select_fusion = (f32[2,128,128]{2,1,0:T(8,128)S(1)}, f32[2,128,128]{2,1,0:T(8,128)}) fusion(f32[2,128,128]{2,1,0:T(8,128)S(1)} %copy-done.5, f32[2,128,128]{2,1,0:T(8,128)S(1)} %collective-permute-done.11, pred[]{:T(512)S(6)} %or.4, f32[2,128,128]{2,1,0:T(8,128)S(1)} %copy-done.4, f32[2,128,128]{2,1,0:T(8,128)S(1)} %collective-permute-done.10), kind=kLoop, calls=%fused_computation.1 | loop fusion | flops 131072 | bytes 786433 | tf_op jit(solution)/shard_map/jit(_where)/select_n | solution.py:264
  37.8 2.0 %collective-permute-start.13 = (f32[2,128,128]{2,1,0:T(8,128)S(1)}, f32[2,128,128]{2,1,0:T(8,128)S(1)}, u32[]{:S(2)}, u32[]{:S(2)}) collective-permute-start(f32[2,128,128]{2,1,0:T(8,128)S(1)} %get-tuple-element.37), channel_id=1, source_target_pairs={{0,1},{1,3},{2,0},{3,2},{4,5},{5,7},{6,4},{7,6},{8,9},{9,11},{10,8... | collective-permute-start | bytes 393224 | tf_op jit(solution)/shard_map/ppermute | solution.py:265
  39.8 5.4 %collective-permute-done.4 = f32[2,128,128]{2,1,0:T(8,128)S(1)} collective-permute-done((f32[2,128,128]{2,1,0:T(8,128)}, f32[2,128,128]{2,1,0:T(8,128)S(1)}, u32[]{:S(2)}, u32[]{:S(2)}) %collective-permute-start.4) | collective-permute-done | bytes 131104 | tf_op jit(solution)/shard_map/ppermute | solution.py:261
  45.2 0.7 %add_select_fusion.1 = (f32[2,128,128]{2,1,0:T(8,128)S(1)}, f32[2,128,128]{2,1,0:T(8,128)}) fusion(f32[2,128,128]{2,1,0:T(8,128)S(1)} %copy-done.7, f32[2,128,128]{2,1,0:T(8,128)S(1)} %collective-permute-done.4, pred[]{:T(512)S(6)} %or.4, f32[2,128,128]{2,1,0:T(8,128)S(1)} %copy-done.6, f32[2,128,128]{2,1,0:T(8,128)S(1)} %collective-permute-done.3), kind=kLoop, calls=%fused_computation.2 | loop fusion | flops 131072 | bytes 786433 | tf_op jit(solution)/shard_map/jit(_where)/select_n | solution.py:264
  45.9 1.1 %collective-permute-start.6 = (f32[2,128,128]{2,1,0:T(8,128)S(1)}, f32[2,128,128]{2,1,0:T(8,128)S(1)}, u32[]{:S(2)}, u32[]{:S(2)}) collective-permute-start(f32[2,128,128]{2,1,0:T(8,128)S(1)} %get-tuple-element.39), channel_id=1, source_target_pairs={{0,1},{1,3},{2,0},{3,2},{4,5},{5,7},{6,4},{7,6},{8,9},{9,11},{10,8... | collective-permute-start | bytes 393224 | tf_op jit(solution)/shard_map/ppermute | solution.py:265
  47.1 0.7 %pad_maximum_fusion.phase = f32[256,256]{1,0:T(8,128)} fusion(f32[256,128]{1,0:T(8,128)S(1)} %collective-permute-done.15, f32[256,128]{1,0:T(8,128)S(1)} %constant_dynamic-update-slice_fusion), kind=kLoop, calls=%fused_computation | loop fusion | flops 65536 | bytes 524288 | tf_op jit(solution)/shard_map/concatenate | solution.py:335
  47.8 2.8 %transmission.1.refs_6_ = f32[2,2,2,128,128]{4,3,2,1,0:T(8,128)} custom-call(f32[256,256]{1,0:T(8,128)} %pad_maximum_fusion.phase, f32[8,8,128]{2,1,0:T(8,128)} %slot_parameters.1.refs_5_.params), custom_call_target="tpu_custom_call" | custom-call | tf_op jit(solution)/shard_map/transmission/pallas_call | solution.py:271
  50.7 1.1 %collective-permute-done.6.refs_2_ = f32[2,128,128]{2,1,0:T(8,128)S(1)} collective-permute-done((f32[2,128,128]{2,1,0:T(8,128)S(1)}, f32[2,128,128]{2,1,0:T(8,128)S(1)}, u32[]{:S(2)}, u32[]{:S(2)}) %collective-permute-start.6) | collective-permute-done | bytes 131104 | tf_op jit(solution)/shard_map/ppermute | solution.py:265
  52.4 2.8 %patterns.1 = f32[1,1,2,128,128]{4,3,2,1,0:T(8,128)} custom-call(f32[2,128,128]{2,1,0:T(8,128)} %get-tuple-element.40.refs_0_, f32[2,128,128]{2,1,0:T(8,128)} %copy-done.1, f32[2,128,128]{2,1,0:T(8,128)} %copy-done.3, f32[2,128,128]{2,1,0:T(8,128)} %get-tuple-element.38.refs_3_, f32[2,128,128]{2,1,0:T(8,128)} %copy-done, f32[2,128,128]{2,1,0:T(8,128)} %copy-done.2, ...), custom_call_target="tpu_custom_call" | custom-call | flops 201326592 | bytes 2097152 | tf_op jit(solution)/shard_map/patterns/pallas_call | solution.py:271
  (66 shorter events, 5.4 us)
Async XLA Ops:
  2.9 15.4 %collective-permute-start.7 = (f32[2,128,128]{2,1,0:T(8,128)}, f32[2,128,128]{2,1,0:T(8,128)S(1)}, u32[]{:S(2)}, u32[]{:S(2)}) collective-permute-start(f32[2,128,128]{2,1,0:T(8,128)} %get-tuple-element.30), channel_id=1, source_target_pairs={{0,4},{4,8},{8,12},{12,0},{1,5},{5,9},{9,13},{13,1},{2,6},{6,10},{... | collective-permute-start | bytes 393224 | tf_op jit(solution)/shard_map/ppermute | solution.py:23
  3.3 15.4 %collective-permute-start.8 = (f32[2,128,128]{2,1,0:T(8,128)}, f32[2,128,128]{2,1,0:T(8,128)S(1)}, u32[]{:S(2)}, u32[]{:S(2)}) collective-permute-start(f32[2,128,128]{2,1,0:T(8,128)} %get-tuple-element.31), channel_id=1, source_target_pairs={{0,8},{4,12},{8,0},{12,4},{1,9},{5,13},{9,1},{13,5},{2,10},{6,14},... | collective-permute-start | bytes 393224 | tf_op jit(solution)/shard_map/ppermute | solution.py:23
  5.8 4.3 %copy-start.14 = (f32[128,128]{1,0:T(8,128)S(1)}, f32[128,128]{1,0:T(8,128)}, u32[]{:S(2)}) copy-start(f32[128,128]{1,0:T(8,128)} %param.19) | copy-start | bytes 196612
  5.8 14.1 %collective-permute-start.9 = (f32[2,128,128]{2,1,0:T(8,128)}, f32[2,128,128]{2,1,0:T(8,128)S(1)}, u32[]{:S(2)}, u32[]{:S(2)}) collective-permute-start(f32[2,128,128]{2,1,0:T(8,128)} %get-tuple-element.32), channel_id=1, source_target_pairs={{0,12},{4,0},{8,4},{12,8},{1,13},{5,1},{9,5},{13,9},{2,14},{6,2},{... | collective-permute-start | bytes 393224 | tf_op jit(solution)/shard_map/ppermute | solution.py:23
  10.1 8.6 %copy-start.19 = (f32[2,128,128]{2,1,0:T(8,128)S(1)}, f32[2,128,128]{2,1,0:T(8,128)}, u32[]{:S(2)}) copy-start(f32[2,128,128]{2,1,0:T(8,128)} %get-tuple-element.24) | copy-start | bytes 393220
  10.1 15.6 %collective-permute-start = (f32[2,128,128]{2,1,0:T(8,128)}, f32[2,128,128]{2,1,0:T(8,128)S(1)}, u32[]{:S(2)}, u32[]{:S(2)}) collective-permute-start(f32[2,128,128]{2,1,0:T(8,128)} %get-tuple-element.22), channel_id=1, source_target_pairs={{0,4},{4,8},{8,12},{12,0},{1,5},{5,9},{9,13},{13,1},{2,6},{6,10},{... | collective-permute-start | bytes 393224 | tf_op jit(solution)/shard_map/ppermute | solution.py:23
  10.1 14.2 %collective-permute-start.14 = (f32[128,128]{1,0:T(8,128)S(1)}, f32[128,128]{1,0:T(8,128)S(1)}, u32[]{:S(2)}, u32[]{:S(2)}) collective-permute-start(f32[128,128]{1,0:T(8,128)S(1)} %copy-done.14), channel_id=1, source_target_pairs={{0,3},{1,0},{2,1},{3,2},{4,7},{5,4},{6,5},{7,6},{8,11},{9,8},{10,9... | collective-permute-start | bytes 196616 | tf_op jit(solution)/shard_map/ppermute | solution.py:23
  18.2 7.6 %collective-permute-start.1 = (f32[2,128,128]{2,1,0:T(8,128)}, f32[2,128,128]{2,1,0:T(8,128)S(1)}, u32[]{:S(2)}, u32[]{:S(2)}) collective-permute-start(f32[2,128,128]{2,1,0:T(8,128)} %get-tuple-element.23), channel_id=1, source_target_pairs={{0,8},{4,12},{8,0},{12,4},{1,9},{5,13},{9,1},{13,5},{2,10},{6,14},... | collective-permute-start | bytes 393224 | tf_op jit(solution)/shard_map/ppermute | solution.py:23
  18.8 9.1 %collective-permute-start.2 = (f32[2,128,128]{2,1,0:T(8,128)S(1)}, f32[2,128,128]{2,1,0:T(8,128)S(1)}, u32[]{:S(2)}, u32[]{:S(2)}) collective-permute-start(f32[2,128,128]{2,1,0:T(8,128)S(1)} %copy-done.19), channel_id=1, source_target_pairs={{0,12},{4,0},{8,4},{12,8},{1,13},{5,1},{9,5},{13,9},{2,14},{6,2},{... | collective-permute-start | bytes 393224 | tf_op jit(solution)/shard_map/ppermute | solution.py:23
  23.6 2.2 %copy-start.18 = (f32[2,128,128]{2,1,0:T(8,128)S(1)}, f32[2,128,128]{2,1,0:T(8,128)}, u32[]{:S(2)}) copy-start(f32[2,128,128]{2,1,0:T(8,128)} %get-tuple-element.34) | copy-start | bytes 393220
  23.6 8.5 %collective-permute-start.10 = (f32[2,128,128]{2,1,0:T(8,128)}, f32[2,128,128]{2,1,0:T(8,128)S(1)}, u32[]{:S(2)}, u32[]{:S(2)}) collective-permute-start(f32[2,128,128]{2,1,0:T(8,128)} %get-tuple-element.34), channel_id=1, source_target_pairs={{1,2},{2,1},{5,6},{6,5},{9,10},{10,9},{13,14},{14,13},{17,18},{18,... | collective-permute-start | bytes 393224 | tf_op jit(solution)/shard_map/ppermute | solution.py:262
  24.4 12.6 %collective-permute-start.11 = (f32[2,128,128]{2,1,0:T(8,128)}, f32[2,128,128]{2,1,0:T(8,128)S(1)}, u32[]{:S(2)}, u32[]{:S(2)}) collective-permute-start(f32[2,128,128]{2,1,0:T(8,128)} %get-tuple-element.35), channel_id=1, source_target_pairs={{0,1},{1,0},{2,3},{3,2},{4,5},{5,4},{6,7},{7,6},{8,9},{9,8},{10,11... | collective-permute-start | bytes 393224 | tf_op jit(solution)/shard_map/ppermute | solution.py:261
  25.7 2.1 %copy-start.8 = (f32[2,128,128]{2,1,0:T(8,128)}, f32[2,128,128]{2,1,0:T(8,128)S(1)}, u32[]{:S(2)}) copy-start(f32[2,128,128]{2,1,0:T(8,128)S(1)} %collective-permute-done.refs_1_) | copy-start | bytes 393220
  25.7 21.3 %collective-permute-start.15 = (f32[256,128]{1,0:T(8,128)S(1)}, f32[256,128]{1,0:T(8,128)S(1)}, u32[]{:S(2)}, u32[]{:S(2)}) collective-permute-start(f32[256,128]{1,0:T(8,128)S(1)} %constant_dynamic-update-slice_fusion), channel_id=1, source_target_pairs={{0,12},{4,0},{8,4},{12,8},{1,13},{5,1},{9,5},{13,9},{2,14},{6,2},{... | collective-permute-start | bytes 393224 | tf_op jit(solution)/shard_map/ppermute | solution.py:23
  25.8 24.8 %collective-permute-start.12 = (f32[2,128,128]{2,1,0:T(8,128)S(1)}, f32[2,128,128]{2,1,0:T(8,128)S(1)}, u32[]{:S(2)}, u32[]{:S(2)}) collective-permute-start(f32[2,128,128]{2,1,0:T(8,128)S(1)} %copy-done.18), channel_id=1, source_target_pairs={{0,2},{3,1},{4,6},{7,5},{8,10},{11,9},{12,14},{15,13},{16,18},{19,... | collective-permute-start | bytes 393224 | tf_op jit(solution)/shard_map/ppermute | solution.py:263
  28.5 8.6 %copy-start.4 = (f32[2,128,128]{2,1,0:T(8,128)S(1)}, f32[2,128,128]{2,1,0:T(8,128)}, u32[]{:S(2)}) copy-start(f32[2,128,128]{2,1,0:T(8,128)} %get-tuple-element.33) | copy-start | bytes 393220
  28.5 8.6 %copy-start.5 = (f32[2,128,128]{2,1,0:T(8,128)S(1)}, f32[2,128,128]{2,1,0:T(8,128)}, u32[]{:S(2)}) copy-start(f32[2,128,128]{2,1,0:T(8,128)} %get-tuple-element.36) | copy-start | bytes 393220
  31.4 6.4 %collective-permute-start.3 = (f32[2,128,128]{2,1,0:T(8,128)}, f32[2,128,128]{2,1,0:T(8,128)S(1)}, u32[]{:S(2)}, u32[]{:S(2)}) collective-permute-start(f32[2,128,128]{2,1,0:T(8,128)} %get-tuple-element.26), channel_id=1, source_target_pairs={{1,2},{2,1},{5,6},{6,5},{9,10},{10,9},{13,14},{14,13},{17,18},{18,... | collective-permute-start | bytes 393224 | tf_op jit(solution)/shard_map/ppermute | solution.py:262
  32.1 18.5 %collective-permute-start.5 = (f32[2,128,128]{2,1,0:T(8,128)}, f32[2,128,128]{2,1,0:T(8,128)S(1)}, u32[]{:S(2)}, u32[]{:S(2)}) collective-permute-start(f32[2,128,128]{2,1,0:T(8,128)} %get-tuple-element.26), channel_id=1, source_target_pairs={{0,2},{3,1},{4,6},{7,5},{8,10},{11,9},{12,14},{15,13},{16,18},{19,... | collective-permute-start | bytes 393224 | tf_op jit(solution)/shard_map/ppermute | solution.py:263
  37.0 8.2 %collective-permute-start.4 = (f32[2,128,128]{2,1,0:T(8,128)}, f32[2,128,128]{2,1,0:T(8,128)S(1)}, u32[]{:S(2)}, u32[]{:S(2)}) collective-permute-start(f32[2,128,128]{2,1,0:T(8,128)} %get-tuple-element.27), channel_id=1, source_target_pairs={{0,1},{1,0},{2,3},{3,2},{4,5},{5,4},{6,7},{7,6},{8,9},{9,8},{10,11... | collective-permute-start | bytes 393224 | tf_op jit(solution)/shard_map/ppermute | solution.py:261
  37.1 8.1 %copy-start.6 = (f32[2,128,128]{2,1,0:T(8,128)S(1)}, f32[2,128,128]{2,1,0:T(8,128)}, u32[]{:S(2)}) copy-start(f32[2,128,128]{2,1,0:T(8,128)} %get-tuple-element.25) | copy-start | bytes 393220
  37.1 8.1 %copy-start.7 = (f32[2,128,128]{2,1,0:T(8,128)S(1)}, f32[2,128,128]{2,1,0:T(8,128)}, u32[]{:S(2)}) copy-start(f32[2,128,128]{2,1,0:T(8,128)} %get-tuple-element.28) | copy-start | bytes 393220
  37.8 12.8 %collective-permute-start.13 = (f32[2,128,128]{2,1,0:T(8,128)S(1)}, f32[2,128,128]{2,1,0:T(8,128)S(1)}, u32[]{:S(2)}, u32[]{:S(2)}) collective-permute-start(f32[2,128,128]{2,1,0:T(8,128)S(1)} %get-tuple-element.37), channel_id=1, source_target_pairs={{0,1},{1,3},{2,0},{3,2},{4,5},{5,7},{6,4},{7,6},{8,9},{9,11},{10,8... | collective-permute-start | bytes 393224 | tf_op jit(solution)/shard_map/ppermute | solution.py:265
  45.9 5.9 %collective-permute-start.6 = (f32[2,128,128]{2,1,0:T(8,128)S(1)}, f32[2,128,128]{2,1,0:T(8,128)S(1)}, u32[]{:S(2)}, u32[]{:S(2)}) collective-permute-start(f32[2,128,128]{2,1,0:T(8,128)S(1)} %get-tuple-element.39), channel_id=1, source_target_pairs={{0,1},{1,3},{2,0},{3,2},{4,5},{5,7},{6,4},{7,6},{8,9},{9,11},{10,8... | collective-permute-start | bytes 393224 | tf_op jit(solution)/shard_map/ppermute | solution.py:265
  (12 other events, 12.4 us)
